TPU v7x, 32 devices: a whole 2x2x4 slice. The times are simulated.
32 devices in a mesh: crops: 2 (over y), rows: 4 (over z), chan: 2 (over x), sub: 2 (over core).
Axes of the slice: x: 2, y: 2, z: 4, core: 2. Of those that a mesh axis runs over, the one named last changes fastest.
Arguments:
- pair: bfloat16 [64, 32, 128], P(('crops', 'rows', 'sub')), parts along dimension 0, may hold values from -6 to 6
- residue_mask: int32 [64], P('crops'), parts along dimension 0, may hold values from 0 to 1, as said below
- in_gain: float32 [2, 128], replicated, may hold values from 0.1 to 1.9
- in_bias: float32 [2, 128], replicated, may hold values from -3 to 3
- projections: bfloat16 [2, 4, 128, 128], P(None, None, None, 'chan'), may hold values from -0.5 to 0.5
- gate_weight: bfloat16 [2, 128, 128], replicated, may hold values from -0.5 to 0.5
- out_gain: float32 [2, 128], replicated, may hold values from 0.1 to 1.9
- out_bias: float32 [2, 128], replicated, may hold values from -3 to 3
- out_weight: bfloat16 [2, 128, 128], replicated, may hold values from -0.5 to 0.5
Outputs:
- pair_out: bfloat16 [64, 32, 128], P(('crops', 'rows', 'sub'), 'chan'), parts along dimension 0
There are 2 independent parts, one for each index of `crops`. A program takes and returns all parts, laid end to end along the dimension named above; an argument that names none is the same for every part. Nothing has to cross between parts.
Inputs may be any that keep to these rules, and one draw needn't show every extreme that they name: `residue_mask`: residue 0 is always present and residue 32 - 1 is always a gap or padding.
All inputs are finite; a program needn't handle non-finite values.
Results may differ from a plain program's by a relative error of at most 0.012.
Values may be sent and summed in bfloat16 or wider, within the bound.
A program may use at most 64 MiB of HBM per device.

v0:
```python
import jax
import jax.numpy as jnp
from jax import lax
from jax.sharding import PartitionSpec as P

epsilon = 1e-05


def normalize(values, reduce_axis):
    centre = jnp.mean(values, axis=reduce_axis, keepdims=True)
    centred = values - centre
    spread = jnp.mean(centred * centred, axis=reduce_axis, keepdims=True)
    return centred * lax.rsqrt(spread + epsilon)


def shards(
    pair, residue_mask, in_gain, in_bias, projections, gate_weight, out_gain, out_bias, out_weight
):
    rows_block = pair.shape[0]
    length = pair.shape[1]
    chan_count = lax.axis_size("chan")
    chan_index = lax.axis_index("chan")
    quarter = length // chan_count
    row_start = lax.axis_index(("rows", "sub")) * rows_block
    mask_float = residue_mask.astype(jnp.float32)
    own_mask = lax.dynamic_slice_in_dim(mask_float, row_start, rows_block)
    pair_mask = own_mask[None, :, None] * mask_float[None, None, :]

    def project(full_rows, layer_index):
        normed = (
            normalize(full_rows.astype(jnp.float32), 2) * in_gain[layer_index]
            + in_bias[layer_index]
        ).astype(jnp.bfloat16)
        projected = jnp.einsum(
            "ikc,qch->qhik", normed, projections[layer_index], preferred_element_type=jnp.float32
        )
        left_edges = (jax.nn.sigmoid(projected[0]) * projected[1] * pair_mask).astype(jnp.bfloat16)
        right_edges = (jax.nn.sigmoid(projected[2]) * projected[3] * pair_mask).astype(jnp.bfloat16)
        return (normed, left_edges, right_edges)

    def finish(triangle, normed, residual, layer_index):
        gathered = lax.all_to_all(triangle, "chan", split_axis=2, concat_axis=0, tiled=True)
        whole_float = gathered.astype(jnp.float32)
        scaled = (
            normalize(whole_float, 0) * out_gain[layer_index][:, None, None]
            + out_bias[layer_index][:, None, None]
        ).astype(jnp.bfloat16)
        update = jnp.einsum(
            "hij,hc->ijc", scaled, out_weight[layer_index], preferred_element_type=jnp.float32
        )
        normed_part = lax.dynamic_slice_in_dim(normed, chan_index * quarter, quarter, 1)
        gating = jax.nn.sigmoid(
            jnp.einsum(
                "ijc,cd->ijd",
                normed_part,
                gate_weight[layer_index],
                preferred_element_type=jnp.float32,
            )
        )
        return (residual.astype(jnp.float32) + gating * update).astype(jnp.bfloat16)

    normed, left_edges, right_edges = project(pair, 0)
    triangle = jnp.einsum(
        "hik,hjk->hij",
        left_edges,
        lax.all_gather(right_edges, ("rows", "sub"), axis=1, tiled=True),
        preferred_element_type=jnp.float32,
    ).astype(jnp.bfloat16)
    own_quarter = lax.dynamic_slice_in_dim(pair, chan_index * quarter, quarter, 1)
    layer_one = finish(triangle, normed, own_quarter, 0)
    full_rows = lax.all_gather(layer_one, "chan", axis=1, tiled=True)
    normed, left_edges, right_edges = project(full_rows, 1)
    left_cols, right_cols = (
        lax.all_to_all(left_edges, ("rows", "sub"), split_axis=2, concat_axis=1, tiled=True),
        lax.all_to_all(right_edges, ("rows", "sub"), split_axis=2, concat_axis=1, tiled=True),
    )
    triangle = jnp.einsum(
        "hki,hkj->hij",
        left_cols,
        lax.all_gather(right_cols, ("rows", "sub"), axis=2, tiled=True),
        preferred_element_type=jnp.float32,
    )
    return finish(triangle.astype(jnp.bfloat16), normed, layer_one, 1)


def solution(mesh):
    placed = (
        P(("crops", "rows", "sub"), None, None),
        P("crops"),
        P(),
        P(),
        P(None, None, None, "chan"),
        P(),
        P(),
        P(),
        P(),
    )
    return jax.shard_map(
        shards,
        mesh=mesh,
        in_specs=placed,
        out_specs=P(("crops", "rows", "sub"), "chan", None),
        check_vma=False,
    )
```

profile of v0, /device:TPU:0, one launch (start us, length us, event | category | flops | bytes accessed | tf_op | source)
XLA Modules:
  0.0 73.9 jit_solution(12154159398881067945)
XLA Ops:
  0.0 0.6 copy-done.8
  0.7 0.1 dynamic_slice.14
  0.7 0.1 broadcast_multiply_fusion.2
  0.8 0.8 %convert_reduce_fusion.1 = f32[4,32]{1,0:T(4,128)S(1)} fusion(bf16[4,32,128]{2,1,0:T(8,128)(2,1)} %param.9), kind=kLoop, calls=%fused_computation.21 | loop fusion | flops 32640 | bytes 33280 | tf_op jit(solution)/shard_map/reduce_sum | solution.py:10
  1.7 0.0 copy-done
  1.7 0.2 fusion.18
  1.9 0.1 fusion.21
  2.0 0.2 convolution_bitcast_fusion.1
  2.2 0.1 fusion.36
  2.3 15.9 %all_gather.9 = bf16[64,32,32]{0,2,1:T(8,128)(2,1)S(1)} all-gather(bf16[64,4,32]{0,2,1:T(8,128)(2,1)S(1)} %get-tuple-element.11), channel_id=1, replica_groups=mesh['crops'=2,'rows'=4,'chan'=2,'sub'=2] {'rows','sub'}, dimensions={1}, use_global_device_ids=true | all-gather | bytes 147456 | tf_op jit(solution)/shard_map/all_gather | solution.py:66
  18.2 0.8 %copy.58 = bf16[64,32,32]{2,1,0:T(8,128)(2,1)S(1)} copy(bf16[64,32,32]{0,2,1:T(8,128)(2,1)S(1)} %all_gather.9) | data formatting | bytes 262144 | tf_op jit(solution)/shard_map/all_gather | solution.py:66
  19.0 0.1 copy.57
  19.1 0.4 convolution_convert_fusion.1
  19.5 0.1 copy.59
  19.6 0.0 copy-start.7
  19.6 0.7 reshape.162
  20.3 3.2 %all-to-all-start = ((bf16[2,2,2048]{2,1,0:T(2,128)(2,1)}), bf16[2,2,2048]{2,1,0:T(2,128)(2,1)S(1)}, u32[]{:S(2)}, u32[]{:S(2)}) async-start(bf16[2,2,2048]{2,1,0:T(2,128)(2,1)} %reshape.162), calls=%async_computation | async-start | bytes 32768 | tf_op jit(solution)/shard_map/all_to_all | solution.py:42
  23.6 0.0 copy-start.5
  23.6 0.0 copy-start.6
  23.6 0.1 fusion.7
  23.8 0.5 copy-done.5
  24.3 0.0 copy-done.6
  24.3 0.1 add.124
  24.4 0.1 mul.183
  24.5 2.9 %all-to-all-done = bf16[2,2,2048]{2,1,0:T(2,128)(2,1)S(1)} async-done(((bf16[2,2,2048]{2,1,0:T(2,128)(2,1)}), bf16[2,2,2048]{2,1,0:T(2,128)(2,1)S(1)}, u32[]{:S(2)}, u32[]{:S(2)}) %all-to-all-start) | async-done | bytes 16416 | tf_op jit(solution)/shard_map/all_to_all | solution.py:42
  27.4 0.1 reshape.163
  27.5 0.1 fusion.60
  27.6 0.2 fusion.63
  27.8 0.1 fusion.66
  27.9 0.0 copy-start.2
  28.0 0.1 convert_element_type.92
  28.1 0.7 copy-done.2
  28.8 0.1 fusion.8
  28.9 4.4 %all_gather.10 = bf16[4,32,128]{2,1,0:T(8,128)(2,1)S(1)} all-gather(bf16[4,16,128]{2,1,0:T(8,128)(2,1)S(1)} %fusion.8), channel_id=1, replica_groups=mesh['crops'=2,'rows'=4,'chan'=2,'sub'=2] {'chan'}, dimensions={1}, use_global_device_ids=true | all-gather | bytes 49152 | tf_op jit(solution)/shard_map/all_gather | solution.py:71
  33.3 0.1 convert_reduce_fusion
  33.4 0.2 fusion.14
  33.6 0.1 fusion.17
  33.7 0.2 convolution_bitcast_fusion
  33.9 0.1 fusion.24
  34.0 0.7 reshape.166
  34.7 4.7 %all-to-all-start.2 = ((bf16[8,2,512]{2,1,0:T(2,128)(2,1)}), bf16[8,2,512]{2,1,0:T(2,128)(2,1)S(1)}, u32[]{:S(2)}, u32[]{:S(2)}) async-start(bf16[8,2,512]{2,1,0:T(2,128)(2,1)} %reshape.166), calls=%async_computation.2 | async-start | bytes 32768 | tf_op jit(solution)/shard_map/all_to_all | solution.py:75
  39.4 0.1 add.136
  39.5 0.1 mul.200
  39.6 0.7 reshape.164
  40.3 4.8 %all-to-all-done.2 = bf16[8,2,512]{2,1,0:T(2,128)(2,1)S(1)} async-done(((bf16[8,2,512]{2,1,0:T(2,128)(2,1)}), bf16[8,2,512]{2,1,0:T(2,128)(2,1)S(1)}, u32[]{:S(2)}, u32[]{:S(2)}) %all-to-all-start.2) | async-done | bytes 16416 | tf_op jit(solution)/shard_map/all_to_all | solution.py:75
  45.1 3.3 %all-to-all-start.1 = ((bf16[8,2,512]{2,1,0:T(2,128)(2,1)}), bf16[8,2,512]{2,1,0:T(2,128)(2,1)S(1)}, u32[]{:S(2)}, u32[]{:S(2)}) async-start(bf16[8,2,512]{2,1,0:T(2,128)(2,1)} %reshape.164), calls=%async_computation.1 | async-start | bytes 32768 | tf_op jit(solution)/shard_map/all_to_all | solution.py:74
  48.4 0.1 reshape.167
  48.5 14.7 %all_gather.11 = bf16[64,32,32]{0,1,2:T(8,128)(2,1)S(1)} all-gather(bf16[64,32,4]{0,1,2:T(8,128)(2,1)S(1)} %bitcast.191), channel_id=1, replica_groups=mesh['crops'=2,'rows'=4,'chan'=2,'sub'=2] {'rows','sub'}, dimensions={2}, use_global_device_ids=true | all-gather | bytes 147456 | tf_op jit(solution)/shard_map/all_gather | solution.py:80
  63.2 0.8 %copy.68 = bf16[64,32,32]{1,2,0:T(8,128)(2,1)S(1)} copy(bf16[64,32,32]{0,1,2:T(8,128)(2,1)S(1)} %all_gather.11) | data formatting | bytes 262144 | tf_op jit(solution)/shard_map/all_gather | solution.py:80
  64.0 0.0 all-to-all-done.1
  64.0 0.1 reshape.165
  64.1 0.1 copy.67
  64.2 0.4 convolution_convert_fusion
  64.6 0.1 copy.69
  64.7 0.7 reshape.168
  65.4 3.2 %all-to-all-start.3 = ((bf16[2,2,2048]{2,1,0:T(2,128)(2,1)}), bf16[2,2,2048]{2,1,0:T(2,128)(2,1)S(1)}, u32[]{:S(2)}, u32[]{:S(2)}) async-start(bf16[2,2,2048]{2,1,0:T(2,128)(2,1)} %reshape.168), calls=%async_computation.3 | async-start | bytes 32768 | tf_op jit(solution)/shard_map/all_to_all | solution.py:42
  68.7 0.1 fusion.3
  68.8 3.7 %all-to-all-done.3 = bf16[2,2,2048]{2,1,0:T(2,128)(2,1)S(1)} async-done(((bf16[2,2,2048]{2,1,0:T(2,128)(2,1)}), bf16[2,2,2048]{2,1,0:T(2,128)(2,1)S(1)}, u32[]{:S(2)}, u32[]{:S(2)}) %all-to-all-start.3) | async-done | bytes 16416 | tf_op jit(solution)/shard_map/all_to_all | solution.py:42
  72.5 0.1 reshape.169
  72.6 0.1 fusion.52
  72.7 0.2 fusion.55
  72.9 0.1 fusion.58
  73.1 0.1 convert_element_type.104
  73.1 0.7 %fusion.9 = bf16[4,16,128]{2,1,0:T(8,128)(2,1)} fusion(f32[4,16,128]{2,1,0:T(8,128)S(1)} %fusion.3, bf16[128,4,16]{0,2,1:T(8,128)(2,1)S(1)} %convert_element_type.104, bf16[2,128,128]{2,1,0:T(8,128)(2,1)S(1)} %copy-done.2, bf16[4,16,128]{2,1,0:T(8,128)(2,1)S(1)} %fusion.8), kind=kOutput, calls=%fused_computation.17 | convolution fusion | flops 2129920 | bytes 114688 | tf_op jit(solution)/shard_map/hij,hc->ijc/dot_general | solution.py:48
  (28 shorter events, 0.2 us)
Async XLA Ops:
  0.0 0.7 copy-start.8
  0.0 1.9 %copy-start.3 = (f32[2,128]{1,0:T(2,128)S(1)}, f32[2,128]{1,0:T(2,128)}, u32[]{:S(2)}) copy-start(f32[2,128]{1,0:T(2,128)} %param.12) | copy-start | bytes 3076
  0.0 1.9 %copy-start.4 = (f32[2,128]{1,0:T(2,128)S(1)}, f32[2,128]{1,0:T(2,128)}, u32[]{:S(2)}) copy-start(f32[2,128]{1,0:T(2,128)} %param.11) | copy-start | bytes 3076
  0.0 1.7 %copy-start = (bf16[4,32,128]{2,1,0:T(8,128)(2,1)S(1)}, bf16[4,32,128]{2,1,0:T(8,128)(2,1)}, u32[]{:S(2)}) copy-start(bf16[4,32,128]{2,1,0:T(8,128)(2,1)} %param.9) | copy-start | bytes 98308
  0.0 2.0 %copy-start.1 = (bf16[2,4,128,64]{2,3,1,0:T(8,128)(2,1)S(1)}, bf16[2,4,128,64]{2,3,1,0:T(8,128)(2,1)}, u32[]{:S(2)}) copy-start(bf16[2,4,128,64]{2,3,1,0:T(8,128)(2,1)} %param.13) | copy-start | bytes 393220
  19.6 4.0 %copy-start.7 = (bf16[2,128,128]{2,1,0:T(8,128)(2,1)S(1)}, bf16[2,128,128]{2,1,0:T(8,128)(2,1)}, u32[]{:S(2)}) copy-start(bf16[2,128,128]{2,1,0:T(8,128)(2,1)} %param.14) | copy-start | bytes 196612
  20.3 7.1 %all-to-all-start = ((bf16[2,2,2048]{2,1,0:T(2,128)(2,1)}), bf16[2,2,2048]{2,1,0:T(2,128)(2,1)S(1)}, u32[]{:S(2)}, u32[]{:S(2)}) async-start(bf16[2,2,2048]{2,1,0:T(2,128)(2,1)} %reshape.162), calls=%async_computation | async-start | bytes 32768 | tf_op jit(solution)/shard_map/all_to_all | solution.py:42
  23.6 0.7 copy-start.5
  23.6 0.7 copy-start.6
  27.9 0.8 %copy-start.2 = (bf16[2,128,128]{2,1,0:T(8,128)(2,1)S(1)}, bf16[2,128,128]{2,1,0:T(8,128)(2,1)}, u32[]{:S(2)}) copy-start(bf16[2,128,128]{2,1,0:T(8,128)(2,1)} %param.17) | copy-start | bytes 196612
  34.7 10.3 %all-to-all-start.2 = ((bf16[8,2,512]{2,1,0:T(2,128)(2,1)}), bf16[8,2,512]{2,1,0:T(2,128)(2,1)S(1)}, u32[]{:S(2)}, u32[]{:S(2)}) async-start(bf16[8,2,512]{2,1,0:T(2,128)(2,1)} %reshape.166), calls=%async_computation.2 | async-start | bytes 32768 | tf_op jit(solution)/shard_map/all_to_all | solution.py:75
  45.1 18.9 %all-to-all-start.1 = ((bf16[8,2,512]{2,1,0:T(2,128)(2,1)}), bf16[8,2,512]{2,1,0:T(2,128)(2,1)S(1)}, u32[]{:S(2)}, u32[]{:S(2)}) async-start(bf16[8,2,512]{2,1,0:T(2,128)(2,1)} %reshape.164), calls=%async_computation.1 | async-start | bytes 32768 | tf_op jit(solution)/shard_map/all_to_all | solution.py:74
  65.4 7.1 %all-to-all-start.3 = ((bf16[2,2,2048]{2,1,0:T(2,128)(2,1)}), bf16[2,2,2048]{2,1,0:T(2,128)(2,1)S(1)}, u32[]{:S(2)}, u32[]{:S(2)}) async-start(bf16[2,2,2048]{2,1,0:T(2,128)(2,1)} %reshape.168), calls=%async_computation.3 | async-start | bytes 32768 | tf_op jit(solution)/shard_map/all_to_all | solution.py:42
where the time goes:
time: 74.4 us; the launch traced here: 73.9 us
  blocking collectives  35 us (47%)
  starting transfers between devices  14.5 us (19%)
  waiting for transfers between devices  11.4 us (15%)
  local copies, waits for them, and re-layouts  7.84 us (11%)
  other arithmetic  2.48 us (3%)
  matrix products  2.32 us (3%)
    all_gather x1, blocking collectives, shards(): lax.all_gather(right_edges, ('rows', 'sub'), axis=1, tiled=True)  15.9 us
    all_gather x1, blocking collectives, shards(): lax.all_gather(right_cols, ('rows', 'sub'), axis=2, tiled=True)  14.7 us
    all_to_all x2, waiting for transfers between devices, finish(): lax.all_to_all(triangle, 'chan', split_axis=2, concat_axis=0, tiled=True)  6.63 us
    all_to_all x2, starting transfers between devices, finish(): lax.all_to_all(triangle, 'chan', split_axis=2, concat_axis=0, tiled=True)  6.47 us
    unnamed x26, local copies, waits for them, and re-layouts  5.09 us
    all_to_all x1, waiting for transfers between devices, shards(): lax.all_to_all(right_edges, ('rows', 'sub'), split_axis=2, concat_axis=1,...  4.77 us
    all_to_all x1, starting transfers between devices, shards(): lax.all_to_all(right_edges, ('rows', 'sub'), split_axis=2, concat_axis=1,...  4.68 us
    all_gather x1, blocking collectives, shards(): full_rows = lax.all_gather(layer_one, 'chan', axis=1, tiled=True)  4.4 us
  transfers between devices with their start and end apart: 4, of which 3 were waited for; matrix products, arithmetic and copies ran while one was open for 3% of the time, Pallas kernels for 0%

commit v1 on v0

v1 whole, which is shorter than its diff:
```python
import functools

import jax
import jax.numpy as jnp
from jax import lax
from jax.experimental import pallas as pl
from jax.experimental.pallas import tpu as pltpu
from jax.sharding import PartitionSpec as P

epsilon = 1e-05
chunk_pixels = 256
MESH = pl.DeviceIdType.MESH


def normalize(values):
    centre = jnp.mean(values, axis=-1, keepdims=True)
    centred = values - centre
    spread = jnp.mean(centred * centred, axis=-1, keepdims=True)
    return centred * lax.rsqrt(spread + epsilon)


def sigmoid(values):
    return 0.5 * jnp.tanh(0.5 * values) + 0.5


def matmul(values, weight):
    flat = values.astype(jnp.bfloat16).reshape(-1, values.shape[-1])
    out = jnp.dot(flat, weight, preferred_element_type=jnp.float32)
    return out.reshape(values.shape[:-1] + (weight.shape[-1],))


def repeat(count, body):
    if count <= 8:
        for step in range(count):
            body(step)
    else:
        lax.fori_loop(0, count, lambda step, _: (body(step), 0)[1], 0)


def kernel(
    sizes,
    pair_ref,
    mask_ref,
    in_gain_ref,
    in_bias_ref,
    proj_ref,
    gate_ref,
    out_gain_ref,
    out_bias_ref,
    weight_ref,
    out_ref,
    left_rows,
    right_rows,
    pieces,
    tiles,
    mine,
    full,
    in_gain,
    in_bias,
    gate,
    out_gain,
    out_bias,
    weight,
    mask_cols,
    residual,
    normed,
    edges,
    triangle,
    edges_one,
    local_sem,
    first_send,
    left_recv,
    right_recv,
    piece_send,
    piece_recv,
    tile_send,
    tile_recv,
):
    zs, chan, sub, block, length = sizes
    chip_rows = sub * block
    width = length // (chan * sub)
    per_tile = width // block
    z, x, s = lax.axis_index("rows"), lax.axis_index("chan"), lax.axis_index("sub")
    own_block = z * sub + s
    tile = s * chan + x
    tile_part, tile_slot = tile // sub, tile % sub

    def device(dz, dx, ds):
        return {"rows": dz, "chan": dx, "sub": ds}

    small = [
        pltpu.make_async_copy(source, target, local_sem.at[index])
        for index, (source, target) in enumerate(
            (
                (pair_ref, left_rows.at[pl.ds(s * block, block)]),
                (proj_ref.at[0], pieces.at[x, 0]),
                (proj_ref.at[1], pieces.at[x, 1]),
                (in_gain_ref, in_gain),
                (in_bias_ref, in_bias),
                (gate_ref, gate),
                (out_gain_ref, out_gain),
                (out_bias_ref, out_bias),
                (weight_ref, weight),
            )
        )
    ]
    for copy in small:
        copy.start()

    barrier = pltpu.get_barrier_semaphore()
    others = chan * sub

    def greet(dz):
        for inner in range(others):
            dx, ds = inner // sub, inner % sub

            def signal():
                pl.semaphore_signal(
                    barrier,
                    inc=1,
                    device_id=device((z + dz) % zs, (x + dx) % chan, (s + ds) % sub),
                    device_id_type=MESH,
                )

            if inner == 0:
                if isinstance(dz, int):
                    if dz != 0:
                        signal()
                else:
                    pl.when(dz != 0)(signal)
            else:
                signal()

    repeat(zs, greet)
    pl.semaphore_wait(barrier, zs * others - 1)

    target_tile = own_block // per_tile
    target_x, target_s = target_tile % chan, target_tile // chan
    slot = own_block % per_tile

    def left_copy(ds):
        return pltpu.make_async_remote_copy(
            src_ref=pair_ref,
            dst_ref=left_rows.at[pl.ds(s * block, block)],
            send_sem=first_send.at[zs + ds - 1],
            recv_sem=left_recv.at[s],
            device_id=device(z, x, (s + ds) % sub),
            device_id_type=MESH,
        )

    def right_copy(dest_z):
        return pltpu.make_async_remote_copy(
            src_ref=pair_ref,
            dst_ref=right_rows.at[pl.ds(slot * block, block)],
            send_sem=first_send.at[dest_z],
            recv_sem=right_recv.at[slot],
            device_id=device(dest_z, x, target_s),
            device_id_type=MESH,
        )

    def sends_right(dest_z):
        return (x == target_x) & ((dest_z != z) | (target_s != s))

    def piece_copy(layer, dx):
        return pltpu.make_async_remote_copy(
            src_ref=proj_ref.at[layer],
            dst_ref=pieces.at[x, layer],
            send_sem=piece_send.at[layer, dx - 1],
            recv_sem=piece_recv.at[layer, x],
            device_id=device(z, (x + dx) % chan, s),
            device_id_type=MESH,
        )

    for dx in range(1, chan):
        piece_copy(0, dx).start()
    repeat(zs, lambda dz: pl.when(sends_right(dz))(lambda: right_copy(dz).start()))
    for ds in range(1, sub):
        left_copy(ds).start()
    for dx in range(1, chan):
        piece_copy(1, dx).start()

    rows_iota = lax.broadcasted_iota(jnp.int32, (length, length), 0)
    cols_iota = lax.broadcasted_iota(jnp.int32, (length, length), 1)
    mask_row = mask_ref[...].astype(jnp.float32)
    mask_col = jnp.sum(jnp.where(rows_iota == cols_iota, mask_row, 0.0), axis=1, keepdims=True)
    mask_cols[...] = jnp.broadcast_to(mask_col, mask_cols.shape)

    for copy in small:
        copy.wait()

    def assemble(layer):
        for other in range(1, chan):
            source = (x + other) % chan
            pltpu.make_async_remote_copy(
                src_ref=proj_ref.at[layer],
                dst_ref=pieces.at[source, layer],
                send_sem=piece_send.at[layer, other - 1],
                recv_sem=piece_recv.at[layer, source],
                device_id=device(z, source, s),
                device_id_type=MESH,
            ).wait_recv()
        for q in range(4):
            full[layer, q] = jnp.concatenate(
                [pieces[c, layer, q] for c in range(chan)], axis=-1
            )

    def scaled_input(values, layer):
        return normalize(values) * in_gain[layer : layer + 1] + in_bias[layer : layer + 1]

    def gated(values, layer, q):
        return sigmoid(matmul(values, full[layer, q])) * matmul(values, full[layer, q + 1])

    def finish(values, normed_part, residual_part, layer):
        whole = values.astype(jnp.bfloat16).astype(jnp.float32)
        scaled = normalize(whole) * out_gain[layer : layer + 1] + out_bias[layer : layer + 1]
        update = matmul(scaled, weight[layer])
        gating = sigmoid(matmul(normed_part, gate[layer]))
        return residual_part + gating * update

    for ds in range(1, sub):
        source = (s + ds) % sub
        pltpu.make_async_remote_copy(
            src_ref=pair_ref,
            dst_ref=left_rows.at[pl.ds(source * block, block)],
            send_sem=first_send.at[zs + ds - 1],
            recv_sem=left_recv.at[source],
            device_id=device(z, x, source),
            device_id_type=MESH,
        ).wait_recv()
    assemble(0)

    step_rows = max(1, min(chunk_pixels // length, chip_rows, width))

    def left_step(step):
        rows = pl.ds(step * step_rows, step_rows)
        values = left_rows[rows].astype(jnp.float32)
        ready = scaled_input(values, 0)
        residual[rows] = values
        normed[rows] = ready
        edges[rows] = gated(ready, 0, 0)

    repeat(chip_rows // step_rows, left_step)

    def right_arrival(p):
        source = tile * per_tile + p
        where = pl.ds(p * block, block)

        @pl.when(source == own_block)
        def _():
            right_rows[where] = left_rows[pl.ds(s * block, block)]

        @pl.when(source != own_block)
        def _():
            pltpu.make_async_remote_copy(
                src_ref=pair_ref,
                dst_ref=right_rows.at[where],
                send_sem=first_send.at[0],
                recv_sem=right_recv.at[p],
                device_id=device(source // sub, x, source % sub),
                device_id_type=MESH,
            ).wait_recv()

    repeat(per_tile, right_arrival)

    def right_step(step):
        rows = pl.ds(step * step_rows, step_rows)
        values = right_rows[rows].astype(jnp.float32)
        right = gated(scaled_input(values, 0), 0, 2) * mask_cols[...]

        def one(i):
            triangle[i, rows] = jnp.sum(right * edges[i], axis=1)

        repeat(chip_rows, one)

    repeat(width // step_rows, right_step)

    columns = pl.ds(pl.multiple_of(tile * width, width), width)
    mask_i = mask_cols[pl.ds(pl.multiple_of(z * chip_rows, chip_rows), chip_rows)]
    masked = triangle[...] * mask_cols[columns] * mask_i.reshape(chip_rows, 1, -1)
    layer_one = finish(masked, normed[:, columns], residual[:, columns], 0).astype(jnp.bfloat16)
    mine[...] = layer_one

    def tile_copy(place, dest, index):
        return pltpu.make_async_remote_copy(
            src_ref=mine,
            dst_ref=tiles.at[place, z],
            send_sem=tile_send.at[index],
            recv_sem=tile_recv.at[place, z],
            device_id=device(*dest),
            device_id_type=MESH,
        )

    def column_target(dz, ds):
        return ((z + dz) % zs, tile_part, (s + ds) % sub)

    def row_target(p, dx):
        target = tile * per_tile + p
        return (target // sub, (tile_part + dx) % chan, target % sub)

    def is_self(dest):
        return (dest[0] == z) & (dest[1] == x) & (dest[2] == s)

    def each_send(act):
        def over_rows(p):
            for dx in range(1, chan):
                dest = row_target(p, dx)
                index = zs * sub + p * (chan - 1) + dx - 1
                pl.when(jnp.logical_not(is_self(dest)))(
                    lambda: act(tile_copy(sub, dest, index))
                )

        def over_columns(dz):
            for ds in range(sub):
                dest = column_target(dz, ds)
                pl.when(jnp.logical_not(is_self(dest)))(
                    lambda: act(tile_copy(tile_slot, dest, dz * sub + ds))
                )

        repeat(zs, over_columns)
        repeat(per_tile, over_rows)

    each_send(lambda copy: copy.start())

    row_tile = own_block // per_tile
    row_part = row_tile // sub
    row_place = jnp.where(row_part == x, row_tile % sub, sub)

    @pl.when(tile_part == x)
    def _():
        tiles[tile_slot, z] = layer_one

    @pl.when((row_tile == tile) & (row_part != x))
    def _():
        tiles[sub, z] = layer_one

    assemble(1)

    def tile_wait(place, source_tile, source_z):
        source = (source_z, source_tile % chan, source_tile // chan)

        @pl.when(jnp.logical_not(is_self(source)))
        def _():
            pltpu.make_async_remote_copy(
                src_ref=mine,
                dst_ref=tiles.at[place, source_z],
                send_sem=tile_send.at[0],
                recv_sem=tile_recv.at[place, source_z],
                device_id=device(*source),
                device_id_type=MESH,
            ).wait_recv()

    for q in range(sub):
        repeat(zs, lambda source_z: tile_wait(q, x * sub + q, source_z))

    @pl.when(row_part != x)
    def _():
        repeat(zs, lambda source_z: tile_wait(sub, row_tile, source_z))

    step_z = max(1, min(chunk_pixels // (chip_rows * width), zs))

    def edge_step(step):
        planes = pl.ds(step * step_z, step_z)
        values = tiles[row_place, planes].astype(jnp.float32)
        edges_one[planes] = gated(scaled_input(values, 1), 1, 0)

    repeat(zs // step_z, edge_step)

    row_offset = (own_block % per_tile) * block
    results = []
    for q in range(sub):

        def tri_step(step, totals):
            planes = pl.ds(step * step_z, step_z)
            values = tiles[q, planes].astype(jnp.float32)
            right = gated(scaled_input(values, 1), 1, 2)
            k_start = step * step_z * chip_rows
            if not isinstance(step, int):
                k_start = pl.multiple_of(k_start, chip_rows)
            mask_k = mask_cols[pl.ds(k_start, step_z * chip_rows)]
            right = right * mask_k.reshape(step_z, chip_rows, 1, -1)
            return tuple(
                total
                + jnp.sum(
                    right * edges_one[planes, :, pl.ds(row_offset + i, 1)], axis=(0, 1)
                )
                for i, total in enumerate(totals)
            )

        totals = tuple(jnp.zeros((width, in_gain.shape[-1]), jnp.float32) for _ in range(block))
        if zs // step_z == 1:
            totals = tri_step(0, totals)
        else:
            totals = lax.fori_loop(0, zs // step_z, tri_step, totals)
        start = pl.multiple_of((x * sub + q) * width, width)
        mask_j = mask_cols[pl.ds(start, width)]
        mask_i = [mask_cols[pl.ds(own_block * block + i, 1)] for i in range(block)]
        masked = jnp.stack([total * mask_j * m for total, m in zip(totals, mask_i)])
        own = tiles[q, z, pl.ds(s * block, block)].astype(jnp.float32)
        results.append(finish(masked, scaled_input(own, 1), own, 1))
    out_ref[...] = jnp.concatenate(results, axis=1).astype(out_ref.dtype)

    for ds in range(1, sub):
        left_copy(ds).wait_send()
    repeat(zs, lambda dz: pl.when(sends_right(dz))(lambda: right_copy(dz).wait_send()))
    for layer in range(2):
        for dx in range(1, chan):
            piece_copy(layer, dx).wait_send()
    each_send(lambda copy: copy.wait_send())


def shards(sizes, pair, residue_mask, in_gain, in_bias, projections, gate_weight, out_gain, out_bias, out_weight):
    zs, chan, sub = sizes
    block, length, channels = pair.shape
    layers, kinds, _, part = projections.shape
    hidden = part * chan
    chip_rows = sub * block
    width = length // (chan * sub)
    per_tile = width // block
    f32, bf16 = jnp.float32, jnp.bfloat16
    dma = pltpu.SemaphoreType.DMA
    hbm = pl.BlockSpec(memory_space=pl.ANY)
    vmem = pl.BlockSpec(memory_space=pltpu.VMEM)
    return pl.pallas_call(
        functools.partial(kernel, (zs, chan, sub, block, length)),
        out_shape=jax.ShapeDtypeStruct((block, length // chan, channels), bf16),
        in_specs=[hbm, vmem] + [hbm] * 7,
        out_specs=vmem,
        scratch_shapes=[
            pltpu.VMEM((chip_rows, length, channels), bf16),
            pltpu.VMEM((width, length, channels), bf16),
            pltpu.VMEM((chan, layers, kinds, channels, part), bf16),
            pltpu.VMEM((sub + 1, zs, chip_rows, width, channels), bf16),
            pltpu.VMEM((chip_rows, width, channels), bf16),
            pltpu.VMEM((layers, kinds, channels, hidden), bf16),
            pltpu.VMEM(in_gain.shape, f32),
            pltpu.VMEM(in_bias.shape, f32),
            pltpu.VMEM(gate_weight.shape, bf16),
            pltpu.VMEM(out_gain.shape, f32),
            pltpu.VMEM(out_bias.shape, f32),
            pltpu.VMEM(out_weight.shape, bf16),
            pltpu.VMEM((length, hidden), f32),
            pltpu.VMEM((chip_rows, length, channels), f32),
            pltpu.VMEM((chip_rows, length, channels), f32),
            pltpu.VMEM((chip_rows, length, hidden), f32),
            pltpu.VMEM((chip_rows, width, hidden), f32),
            pltpu.VMEM((zs, chip_rows, width, hidden), f32),
            dma((9,)),
            dma((zs + sub,)),
            dma((sub,)),
            dma((per_tile,)),
            dma((layers, chan)),
            dma((layers, chan)),
            dma((zs * sub + per_tile * chan,)),
            dma((sub + 1, zs)),
        ],
        compiler_params=pltpu.CompilerParams(
            collective_id=0, has_side_effects=True, vmem_limit_bytes=56 * 2**20
        ),
    )(
        pair,
        residue_mask.reshape(1, length),
        in_gain,
        in_bias,
        projections,
        gate_weight,
        out_gain,
        out_bias,
        out_weight,
    )


def solution(mesh):
    sizes = (mesh.shape["rows"], mesh.shape["chan"], mesh.shape["sub"])
    placed = (
        P(("crops", "rows", "sub"), None, None),
        P("crops"),
        P(),
        P(),
        P(None, None, None, "chan"),
        P(),
        P(),
        P(),
        P(),
    )
    return jax.shard_map(
        functools.partial(shards, sizes),
        mesh=mesh,
        in_specs=placed,
        out_specs=P(("crops", "rows", "sub"), "chan", None),
        check_vma=False,
    )
```

time: 74.4 us -> 22.7 us (0.31)
  blocking collectives: 35 us -> 0 us
  Pallas kernels: 0 us -> 19.4 us
  starting transfers between devices: 14.5 us -> 0 us
  waiting for transfers between devices: 11.4 us -> 0 us
  local copies, waits for them, and re-layouts: 7.84 us -> 3.06 us
  other arithmetic: 2.48 us -> 0 us
  matrix products: 2.32 us -> 0 us
    all_gather x3 -> x0, blocking collectives: 35 us -> none  [the longest x1 15.9 us: shards(): lax.all_gather(right_edges, ('rows', 'sub'), axis=1, tiled=True)]
    pallas_call x0 -> x1, Pallas kernels: none -> 19.4 us  [shards(): pl.pallas_call(functools.partial(kernel, (zs, chan, sub, block, length)),...]
    all_to_all x4 -> x0, starting transfers between devices: 14.5 us -> none  [the longest x2 6.47 us: finish(): lax.all_to_all(triangle, 'chan', split_axis=2, concat_axis=0, tiled=True)]
    all_to_all x4 -> x0, waiting for transfers between devices: 11.4 us -> none  [the longest x2 6.63 us: finish(): lax.all_to_all(triangle, 'chan', split_axis=2, concat_axis=0, tiled=True)]
    dot_general x8 -> x0, matrix products: 2.32 us -> none  [the longest x2 0.87 us: finish(): jnp.einsum('hij,hc->ijc', scaled, out_weight[layer_index], preferred_elem...]
    unnamed x26 -> x2, local copies, waits for them, and re-layouts: 5.09 us -> 3.06 us
    reduce_sum x8 -> x0, other arithmetic: 1.76 us -> none  [the longest x4 1.12 us: normalize(): centre = jnp.mean(values, axis=reduce_axis, keepdims=True)]
    all_gather x2 -> x0, local copies, waits for them, and re-layouts: 1.55 us -> none  [the longest x1 0.77 us: shards(): lax.all_gather(right_edges, ('rows', 'sub'), axis=1, tiled=True)]
  transfers between devices with their start and end apart: 4 -> 0, of which waited for: 3 -> 0; matrix products, arithmetic and copies ran while one was open for 3% -> 0% of each run, Pallas kernels for 0% -> 0%
where the time goes in v1:
time: 22.7 us; the launch traced here: 22.5 us
  Pallas kernels  19.4 us (85%)
  local copies, waits for them, and re-layouts  3.06 us (13%)
    pallas_call x1, Pallas kernels, shards(): pl.pallas_call(functools.partial(kernel, (zs, chan, sub, block, length)),...  19.4 us
    unnamed x2, local copies, waits for them, and re-layouts  3.06 us

profile of v1, /device:TPU:0, one launch (start us, length us, event | category | flops | bytes accessed | tf_op | source)
XLA Modules:
  0.0 22.5 jit_solution(18208689550772657046)
XLA Ops:
  0.0 1.7 %copy.10.proj_ref = bf16[2,4,128,64]{3,2,1,0:T(8,128)(2,1)} copy(bf16[2,4,128,64]{2,3,1,0:T(8,128)(2,1)} %param.13) | data formatting | bytes 262144 | tf_op args[4]
  1.7 19.4 %shard_map.91 = bf16[4,16,128]{2,1,0:T(8,128)(2,1)} custom-call(bf16[4,32,128]{2,1,0:T(8,128)(2,1)} %pair_ref.1, s32[1,32]{1,0:T(1,128)} %bitcast.1, f32[2,128]{1,0:T(2,128)} %in_gain_ref.1, f32[2,128]{1,0:T(2,128)} %in_bias_ref.1, bf16[2,4,128,64]{3,2,1,0:T(8,128)(2,1)} %copy.10.proj_ref, bf16[2,128,128]{2,1,0:T(8,128)(2,1)} %gate_ref.1, ...), custom_call_target="tpu_custom_call" | custom-call | tf_op jit(solution)/shard_map/pallas_call | solution.py:423
  21.1 1.3 %copy.12 = bf16[4,16,128]{2,1,0:T(8,128)(2,1)} copy(bf16[4,16,128]{2,1,0:T(8,128)(2,1)} %shard_map.91) | data formatting | bytes 32768

commit v2 on v1

--- a/solution.py
+++ b/solution.py
@@ -27,6 +27,14 @@
     flat = values.astype(jnp.bfloat16).reshape(-1, values.shape[-1])
     out = jnp.dot(flat, weight, preferred_element_type=jnp.float32)
     return out.reshape(values.shape[:-1] + (weight.shape[-1],))
+
+
+def matmul_transposed(values, weight):
+    flat = values.astype(jnp.bfloat16).reshape(-1, values.shape[-1])
+    out = lax.dot_general(
+        flat, weight, (((1,), (1,)), ((), ())), preferred_element_type=jnp.float32
+    )
+    return out.reshape(values.shape[:-1] + (weight.shape[0],))
 
 
 def repeat(count, body):
@@ -51,7 +59,6 @@
     out_ref,
     left_rows,
     right_rows,
-    pieces,
     tiles,
     mine,
     full,
@@ -88,13 +95,16 @@
     def device(dz, dx, ds):
         return {"rows": dz, "chan": dx, "sub": ds}
 
+    part = proj_ref.shape[2]
+    own_part = pl.ds(pl.multiple_of(x * part, part), part)
+
     small = [
         pltpu.make_async_copy(source, target, local_sem.at[index])
         for index, (source, target) in enumerate(
             (
                 (pair_ref, left_rows.at[pl.ds(s * block, block)]),
-                (proj_ref.at[0], pieces.at[x, 0]),
-                (proj_ref.at[1], pieces.at[x, 1]),
+                (proj_ref.at[0], full.at[0, :, own_part]),
+                (proj_ref.at[1], full.at[1, :, own_part]),
                 (in_gain_ref, in_gain),
                 (in_bias_ref, in_bias),
                 (gate_ref, gate),
@@ -164,7 +174,7 @@
     def piece_copy(layer, dx):
         return pltpu.make_async_remote_copy(
             src_ref=proj_ref.at[layer],
-            dst_ref=pieces.at[x, layer],
+            dst_ref=full.at[layer, :, own_part],
             send_sem=piece_send.at[layer, dx - 1],
             recv_sem=piece_recv.at[layer, x],
             device_id=device(z, (x + dx) % chan, s),
@@ -193,22 +203,19 @@
             source = (x + other) % chan
             pltpu.make_async_remote_copy(
                 src_ref=proj_ref.at[layer],
-                dst_ref=pieces.at[source, layer],
+                dst_ref=full.at[layer, :, pl.ds(pl.multiple_of(source * part, part), part)],
                 send_sem=piece_send.at[layer, other - 1],
                 recv_sem=piece_recv.at[layer, source],
                 device_id=device(z, source, s),
                 device_id_type=MESH,
             ).wait_recv()
-        for q in range(4):
-            full[layer, q] = jnp.concatenate(
-                [pieces[c, layer, q] for c in range(chan)], axis=-1
-            )
 
     def scaled_input(values, layer):
         return normalize(values) * in_gain[layer : layer + 1] + in_bias[layer : layer + 1]
 
     def gated(values, layer, q):
-        return sigmoid(matmul(values, full[layer, q])) * matmul(values, full[layer, q + 1])
+        gate_part = matmul_transposed(values, full[layer, q])
+        return sigmoid(gate_part) * matmul_transposed(values, full[layer, q + 1])
 
     def finish(values, normed_part, residual_part, layer):
         whole = values.astype(jnp.bfloat16).astype(jnp.float32)
@@ -411,7 +418,8 @@
 def shards(sizes, pair, residue_mask, in_gain, in_bias, projections, gate_weight, out_gain, out_bias, out_weight):
     zs, chan, sub = sizes
     block, length, channels = pair.shape
-    layers, kinds, _, part = projections.shape
+    projections = jnp.swapaxes(projections, 2, 3)
+    layers, kinds, part, _ = projections.shape
     hidden = part * chan
     chip_rows = sub * block
     width = length // (chan * sub)
@@ -428,10 +436,9 @@
         scratch_shapes=[
             pltpu.VMEM((chip_rows, length, channels), bf16),
             pltpu.VMEM((width, length, channels), bf16),
-            pltpu.VMEM((chan, layers, kinds, channels, part), bf16),
             pltpu.VMEM((sub + 1, zs, chip_rows, width, channels), bf16),
             pltpu.VMEM((chip_rows, width, channels), bf16),
-            pltpu.VMEM((layers, kinds, channels, hidden), bf16),
+            pltpu.VMEM((layers, kinds, hidden, channels), bf16),
             pltpu.VMEM(in_gain.shape, f32),
             pltpu.VMEM(in_bias.shape, f32),
             pltpu.VMEM(gate_weight.shape, bf16),

time: 22.7 us -> 20.2 us (0.89)
  local copies, waits for them, and re-layouts: 3.06 us -> 1.32 us
  Pallas kernels: 19.4 us -> 18.6 us
    unnamed x2 -> x1, local copies, waits for them, and re-layouts: 3.06 us -> 1.32 us
    pallas_call x1, Pallas kernels: 19.4 us -> 18.6 us  [shards(): pl.pallas_call(functools.partial(kernel, (zs, chan, sub, block, length)),...]
where the time goes in v2:
time: 20.2 us; the launch traced here: 19.9 us
  Pallas kernels  18.6 us (92%)
  local copies, waits for them, and re-layouts  1.32 us (7%)
    pallas_call x1, Pallas kernels, shards(): pl.pallas_call(functools.partial(kernel, (zs, chan, sub, block, length)),...  18.6 us
    unnamed x1, local copies, waits for them, and re-layouts  1.32 us

profile of v2, /device:TPU:0, one launch (start us, length us, event | category | flops | bytes accessed | tf_op | source)
XLA Modules:
  0.0 19.9 jit_solution(8243158668721528558)
XLA Ops:
  0.0 18.6 %shard_map.91 = bf16[4,16,128]{2,1,0:T(8,128)(2,1)} custom-call(bf16[4,32,128]{2,1,0:T(8,128)(2,1)} %pair_ref.1, s32[1,32]{1,0:T(1,128)} %bitcast.3, f32[2,128]{1,0:T(2,128)} %in_gain_ref.1, f32[2,128]{1,0:T(2,128)} %in_bias_ref.1, bf16[2,4,64,128]{3,2,1,0:T(8,128)(2,1)} %bitcast.2, bf16[2,128,128]{2,1,0:T(8,128)(2,1)} %gate_ref.1, f32[2,128]{1,0:T(2,128)} %out_gain_ref.1, ...), custom_call_target="tpu_custom_call" | custom-call | tf_op jit(solution)/shard_map/pallas_call | solution.py:431
  18.6 1.3 %copy.11 = bf16[4,16,128]{2,1,0:T(8,128)(2,1)} copy(bf16[4,16,128]{2,1,0:T(8,128)(2,1)} %shard_map.91) | data formatting | bytes 32768

commit v3 on v2

--- a/solution.py
+++ b/solution.py
@@ -60,7 +60,6 @@
     left_rows,
     right_rows,
     tiles,
-    mine,
     full,
     in_gain,
     in_bias,
@@ -75,13 +74,17 @@
     triangle,
     edges_one,
     local_sem,
-    first_send,
+    left_send,
     left_recv,
+    right_send,
     right_recv,
     piece_send,
     piece_recv,
     tile_send,
+    relay_send,
+    row_send,
     tile_recv,
+    wave,
 ):
     zs, chan, sub, block, length = sizes
     chip_rows = sub * block
@@ -89,8 +92,8 @@
     per_tile = width // block
     z, x, s = lax.axis_index("rows"), lax.axis_index("chan"), lax.axis_index("sub")
     own_block = z * sub + s
-    tile = s * chan + x
-    tile_part, tile_slot = tile // sub, tile % sub
+    tile = x * sub + s
+    last = zs - 1
 
     def device(dz, dx, ds):
         return {"rows": dz, "chan": dx, "sub": ds}
@@ -118,58 +121,63 @@
         copy.start()
 
     barrier = pltpu.get_barrier_semaphore()
-    others = chan * sub
-
-    def greet(dz):
-        for inner in range(others):
-            dx, ds = inner // sub, inner % sub
-
-            def signal():
-                pl.semaphore_signal(
-                    barrier,
-                    inc=1,
-                    device_id=device((z + dz) % zs, (x + dx) % chan, (s + ds) % sub),
-                    device_id_type=MESH,
-                )
-
-            if inner == 0:
-                if isinstance(dz, int):
-                    if dz != 0:
-                        signal()
-                else:
-                    pl.when(dz != 0)(signal)
-            else:
-                signal()
-
-    repeat(zs, greet)
-    pl.semaphore_wait(barrier, zs * others - 1)
+
+    def greet(*place):
+        pl.semaphore_signal(
+            barrier, inc=1, device_id=device(*place), device_id_type=MESH
+        )
+
+    for inner in range(1, chan * sub):
+        greet(z, (x + inner // sub) % chan, (s + inner % sub) % sub)
+    for ds in range(sub):
+        pl.when(z > 0)(lambda: greet(z - 1, x, (s + ds) % sub))
+        pl.when(z < last)(lambda: greet(z + 1, x, (s + ds) % sub))
+    sides = jnp.where(z > 0, sub, 0) + jnp.where(z < last, sub, 0)
+    pl.semaphore_wait(barrier, chan * sub - 1 + sides)
 
     target_tile = own_block // per_tile
-    target_x, target_s = target_tile % chan, target_tile // chan
+    target_x, target_s = target_tile // sub, target_tile % sub
     slot = own_block % per_tile
 
     def left_copy(ds):
         return pltpu.make_async_remote_copy(
             src_ref=pair_ref,
             dst_ref=left_rows.at[pl.ds(s * block, block)],
-            send_sem=first_send.at[zs + ds - 1],
+            send_sem=left_send.at[ds],
             recv_sem=left_recv.at[s],
             device_id=device(z, x, (s + ds) % sub),
             device_id_type=MESH,
         )
 
-    def right_copy(dest_z):
+    def right_copy(step):
         return pltpu.make_async_remote_copy(
             src_ref=pair_ref,
             dst_ref=right_rows.at[pl.ds(slot * block, block)],
-            send_sem=first_send.at[dest_z],
+            send_sem=right_send.at[per_tile + (step + 1) // 2],
             recv_sem=right_recv.at[slot],
-            device_id=device(dest_z, x, target_s),
+            device_id=device(z + step, x, target_s),
             device_id_type=MESH,
         )
 
-    def sends_right(dest_z):
-        return (x == target_x) & ((dest_z != z) | (target_s != s))
+    def each_right(act):
+        pl.when((x == target_x) & (z < last))(lambda: act(right_copy(1)))
+        pl.when((x == target_x) & (z > 0))(lambda: act(right_copy(-1)))
+
+    def forward_copy(p, step):
+        where = pl.ds(p * block, block)
+        return pltpu.make_async_remote_copy(
+            src_ref=right_rows.at[where],
+            dst_ref=right_rows.at[where],
+            send_sem=right_send.at[p],
+            recv_sem=right_recv.at[p],
+            device_id=device(z + step, x, s),
+            device_id_type=MESH,
+        )
+
+    def each_forward(p, act):
+        source_z = (tile * per_tile + p) // sub
+        pl.when((z > source_z) & (z < last))(lambda: act(forward_copy(p, 1)))
+        pl.when((z < source_z) & (z > 0))(lambda: act(forward_copy(p, -1)))
 
     def piece_copy(layer, dx):
         return pltpu.make_async_remote_copy(
@@ -181,13 +189,24 @@
             device_id_type=MESH,
         )
 
-    for dx in range(1, chan):
-        piece_copy(0, dx).start()
-    repeat(zs, lambda dz: pl.when(sends_right(dz))(lambda: right_copy(dz).start()))
+    each_right(lambda copy: copy.start())
     for ds in range(1, sub):
         left_copy(ds).start()
-    for dx in range(1, chan):
-        piece_copy(1, dx).start()
+    for layer in range(2):
+        for dx in range(1, chan):
+            piece_copy(layer, dx).start()
+
+    @pl.when((z == 0) & (z < last))
+    def _():
+        pl.semaphore_signal(
+            wave.at[0], inc=1, device_id=device(z + 1, x, s), device_id_type=MESH
+        )
+
+    @pl.when((z == last) & (z > 0))
+    def _():
+        pl.semaphore_signal(
+            wave.at[1], inc=1, device_id=device(z - 1, x, s), device_id_type=MESH
+        )
 
     rows_iota = lax.broadcasted_iota(jnp.int32, (length, length), 0)
     cols_iota = lax.broadcasted_iota(jnp.int32, (length, length), 1)
@@ -229,11 +248,48 @@
         pltpu.make_async_remote_copy(
             src_ref=pair_ref,
             dst_ref=left_rows.at[pl.ds(source * block, block)],
-            send_sem=first_send.at[zs + ds - 1],
+            send_sem=left_send.at[ds],
             recv_sem=left_recv.at[source],
             device_id=device(z, x, source),
             device_id_type=MESH,
         ).wait_recv()
+
+    def right_arrival(p):
+        source = tile * per_tile + p
+        where = pl.ds(p * block, block)
+
+        @pl.when(source // sub == z)
+        def _():
+            right_rows[where] = left_rows[pl.ds((source % sub) * block, block)]
+
+        @pl.when(source // sub != z)
+        def _():
+            forward_copy(p, 0).wait_recv()
+
+        each_forward(p, lambda copy: copy.start())
+
+    repeat(per_tile, right_arrival)
+
+    @pl.when(z > 0)
+    def _():
+        pl.semaphore_wait(wave.at[0], 1)
+
+        @pl.when(z < last)
+        def _():
+            pl.semaphore_signal(
+                wave.at[0], inc=1, device_id=device(z + 1, x, s), device_id_type=MESH
+            )
+
+    @pl.when(z < last)
+    def _():
+        pl.semaphore_wait(wave.at[1], 1)
+
+        @pl.when(z > 0)
+        def _():
+            pl.semaphore_signal(
+                wave.at[1], inc=1, device_id=device(z - 1, x, s), device_id_type=MESH
+            )
+
     assemble(0)
 
     step_rows = max(1, min(chunk_pixels // length, chip_rows, width))
@@ -248,27 +304,6 @@
 
     repeat(chip_rows // step_rows, left_step)
 
-    def right_arrival(p):
-        source = tile * per_tile + p
-        where = pl.ds(p * block, block)
-
-        @pl.when(source == own_block)
-        def _():
-            right_rows[where] = left_rows[pl.ds(s * block, block)]
-
-        @pl.when(source != own_block)
-        def _():
-            pltpu.make_async_remote_copy(
-                src_ref=pair_ref,
-                dst_ref=right_rows.at[where],
-                send_sem=first_send.at[0],
-                recv_sem=right_recv.at[p],
-                device_id=device(source // sub, x, source % sub),
-                device_id_type=MESH,
-            ).wait_recv()
-
-    repeat(per_tile, right_arrival)
-
     def right_step(step):
         rows = pl.ds(step * step_rows, step_rows)
         values = right_rows[rows].astype(jnp.float32)
@@ -285,83 +320,70 @@
     mask_i = mask_cols[pl.ds(pl.multiple_of(z * chip_rows, chip_rows), chip_rows)]
     masked = triangle[...] * mask_cols[columns] * mask_i.reshape(chip_rows, 1, -1)
     layer_one = finish(masked, normed[:, columns], residual[:, columns], 0).astype(jnp.bfloat16)
-    mine[...] = layer_one
-
-    def tile_copy(place, dest, index):
+    tiles[s, z] = layer_one
+
+    def tile_copy(place, source_z, send_sem, dest, source_place=s):
         return pltpu.make_async_remote_copy(
-            src_ref=mine,
-            dst_ref=tiles.at[place, z],
-            send_sem=tile_send.at[index],
-            recv_sem=tile_recv.at[place, z],
+            src_ref=tiles.at[source_place, source_z],
+            dst_ref=tiles.at[place, source_z],
+            send_sem=send_sem,
+            recv_sem=tile_recv.at[place, source_z],
             device_id=device(*dest),
             device_id_type=MESH,
         )
 
-    def column_target(dz, ds):
-        return ((z + dz) % zs, tile_part, (s + ds) % sub)
-
-    def row_target(p, dx):
-        target = tile * per_tile + p
-        return (target // sub, (tile_part + dx) % chan, target % sub)
-
-    def is_self(dest):
-        return (dest[0] == z) & (dest[1] == x) & (dest[2] == s)
-
-    def each_send(act):
+    def by_distance(act, distance):
+        pl.when(z + distance < zs)(lambda: act(z + distance))
+        pl.when(z - distance >= 0)(lambda: act(z - distance))
+
+    def each_line(act):
+        repeat(
+            zs - 1,
+            lambda step: by_distance(
+                lambda dest_z: act(tile_copy(s, z, tile_send.at[dest_z], (dest_z, x, s))),
+                zs - 1 - step,
+            ),
+        )
+
+    def each_relay(source_z, act):
+        for ds in range(1, sub):
+            act(tile_copy(s, source_z, relay_send.at[ds, source_z], (z, x, (s + ds) % sub)))
+
+    def each_row(act):
         def over_rows(p):
+            target = tile * per_tile + p
             for dx in range(1, chan):
-                dest = row_target(p, dx)
-                index = zs * sub + p * (chan - 1) + dx - 1
-                pl.when(jnp.logical_not(is_self(dest)))(
-                    lambda: act(tile_copy(sub, dest, index))
-                )
-
-        def over_columns(dz):
-            for ds in range(sub):
-                dest = column_target(dz, ds)
-                pl.when(jnp.logical_not(is_self(dest)))(
-                    lambda: act(tile_copy(tile_slot, dest, dz * sub + ds))
-                )
-
-        repeat(zs, over_columns)
+                dest = (target // sub, (x + dx) % chan, target % sub)
+                act(tile_copy(sub, z, row_send.at[p, dx], dest))
+
         repeat(per_tile, over_rows)
 
-    each_send(lambda copy: copy.start())
+    def start(copy):
+        copy.start()
+
+    each_line(start)
+    each_relay(z, start)
+    each_row(start)
 
     row_tile = own_block // per_tile
     row_part = row_tile // sub
     row_place = jnp.where(row_part == x, row_tile % sub, sub)
-
-    @pl.when(tile_part == x)
-    def _():
-        tiles[tile_slot, z] = layer_one
-
-    @pl.when((row_tile == tile) & (row_part != x))
-    def _():
-        tiles[sub, z] = layer_one
-
     assemble(1)
 
-    def tile_wait(place, source_tile, source_z):
-        source = (source_z, source_tile % chan, source_tile // chan)
-
-        @pl.when(jnp.logical_not(is_self(source)))
-        def _():
-            pltpu.make_async_remote_copy(
-                src_ref=mine,
-                dst_ref=tiles.at[place, source_z],
-                send_sem=tile_send.at[0],
-                recv_sem=tile_recv.at[place, source_z],
-                device_id=device(*source),
-                device_id_type=MESH,
-            ).wait_recv()
-
-    for q in range(sub):
-        repeat(zs, lambda source_z: tile_wait(q, x * sub + q, source_z))
+    def tile_wait(place, source_z):
+        tile_copy(place, source_z, tile_send.at[0], (z, x, s)).wait_recv()
+
+    def line_arrival(source_z):
+        tile_wait(s, source_z)
+        each_relay(source_z, start)
+
+    repeat(zs - 1, lambda step: by_distance(line_arrival, step + 1))
+    for ds in range(1, sub):
+        repeat(zs, lambda source_z: tile_wait((s + ds) % sub, source_z))
 
     @pl.when(row_part != x)
     def _():
-        repeat(zs, lambda source_z: tile_wait(sub, row_tile, source_z))
+        repeat(zs, lambda source_z: tile_wait(sub, source_z))
 
     step_z = max(1, min(chunk_pixels // (chip_rows * width), zs))
 
@@ -408,11 +430,18 @@
 
     for ds in range(1, sub):
         left_copy(ds).wait_send()
-    repeat(zs, lambda dz: pl.when(sends_right(dz))(lambda: right_copy(dz).wait_send()))
+    each_right(lambda copy: copy.wait_send())
+    repeat(per_tile, lambda p: each_forward(p, lambda copy: copy.wait_send()))
     for layer in range(2):
         for dx in range(1, chan):
             piece_copy(layer, dx).wait_send()
-    each_send(lambda copy: copy.wait_send())
+
+    def wait_send(copy):
+        copy.wait_send()
+
+    each_line(wait_send)
+    repeat(zs, lambda source_z: each_relay(source_z, wait_send))
+    each_row(wait_send)
 
 
 def shards(sizes, pair, residue_mask, in_gain, in_bias, projections, gate_weight, out_gain, out_bias, out_weight):
@@ -437,7 +466,6 @@
             pltpu.VMEM((chip_rows, length, channels), bf16),
             pltpu.VMEM((width, length, channels), bf16),
             pltpu.VMEM((sub + 1, zs, chip_rows, width, channels), bf16),
-            pltpu.VMEM((chip_rows, width, channels), bf16),
             pltpu.VMEM((layers, kinds, hidden, channels), bf16),
             pltpu.VMEM(in_gain.shape, f32),
             pltpu.VMEM(in_bias.shape, f32),
@@ -452,13 +480,17 @@
             pltpu.VMEM((chip_rows, width, hidden), f32),
             pltpu.VMEM((zs, chip_rows, width, hidden), f32),
             dma((9,)),
-            dma((zs + sub,)),
             dma((sub,)),
+            dma((sub,)),
+            dma((per_tile + 2,)),
             dma((per_tile,)),
             dma((layers, chan)),
             dma((layers, chan)),
-            dma((zs * sub + per_tile * chan,)),
+            dma((zs,)),
+            dma((sub, zs)),
+            dma((per_tile, chan)),
             dma((sub + 1, zs)),
+            pltpu.SemaphoreType.REGULAR((2,)),
         ],
         compiler_params=pltpu.CompilerParams(
             collective_id=0, has_side_effects=True, vmem_limit_bytes=56 * 2**20

time: 20.2 us -> 22.1 us (1.094)
  the two profiles are of different devices: /device:TPU:0 before, /device:TPU:1 now
where the time goes in v3:
time: 22.1 us; the launch traced here: 21.8 us
  Pallas kernels  20.5 us (93%)
  local copies, waits for them, and re-layouts  1.32 us (6%)
    pallas_call x1, Pallas kernels, shards(): pl.pallas_call(functools.partial(kernel, (zs, chan, sub, block, length)),...  20.5 us
    unnamed x1, local copies, waits for them, and re-layouts  1.32 us

profile of v3, /device:TPU:1, one launch (start us, length us, event | category | flops | bytes accessed | tf_op | source)
XLA Modules:
  0.0 21.8 jit_solution(5588241313021326825)
XLA Ops:
  0.0 20.5 %shard_map.91 = bf16[4,16,128]{2,1,0:T(8,128)(2,1)} custom-call(bf16[4,32,128]{2,1,0:T(8,128)(2,1)} %pair_ref.1, s32[1,32]{1,0:T(1,128)} %bitcast.3, f32[2,128]{1,0:T(2,128)} %in_gain_ref.1, f32[2,128]{1,0:T(2,128)} %in_bias_ref.1, bf16[2,4,64,128]{3,2,1,0:T(8,128)(2,1)} %bitcast.2, bf16[2,128,128]{2,1,0:T(8,128)(2,1)} %gate_ref.1, f32[2,128]{1,0:T(2,128)} %out_gain_ref.1, ...), custom_call_target="tpu_custom_call" | custom-call | tf_op jit(solution)/shard_map/pallas_call | solution.py:460
  20.5 1.3 %copy.11 = bf16[4,16,128]{2,1,0:T(8,128)(2,1)} copy(bf16[4,16,128]{2,1,0:T(8,128)(2,1)} %shard_map.91) | data formatting | bytes 32768

commit v4 on v2

--- a/solution.py
+++ b/solution.py
@@ -98,6 +98,15 @@
     part = proj_ref.shape[2]
     own_part = pl.ds(pl.multiple_of(x * part, part), part)
 
+    def farthest_first(act):
+        def at_distance(step):
+            distance = zs - 1 - step
+            pl.when(z + distance < zs)(lambda: act(z + distance))
+            pl.when(z - distance >= 0)(lambda: act(z - distance))
+
+        repeat(zs - 1, at_distance)
+        act(z)
+
     small = [
         pltpu.make_async_copy(source, target, local_sem.at[index])
         for index, (source, target) in enumerate(
@@ -183,7 +192,11 @@
 
     for dx in range(1, chan):
         piece_copy(0, dx).start()
-    repeat(zs, lambda dz: pl.when(sends_right(dz))(lambda: right_copy(dz).start()))
+
+    def start_right(dest_z):
+        pl.when(sends_right(dest_z))(lambda: right_copy(dest_z).start())
+
+    farthest_first(start_right)
     for ds in range(1, sub):
         left_copy(ds).start()
     for dx in range(1, chan):
@@ -297,8 +310,8 @@
             device_id_type=MESH,
         )
 
-    def column_target(dz, ds):
-        return ((z + dz) % zs, tile_part, (s + ds) % sub)
+    def column_target(dest_z, ds):
+        return (dest_z, tile_part, (s + ds) % sub)
 
     def row_target(p, dx):
         target = tile * per_tile + p
@@ -316,14 +329,14 @@
                     lambda: act(tile_copy(sub, dest, index))
                 )
 
-        def over_columns(dz):
+        def over_columns(dest_z):
             for ds in range(sub):
-                dest = column_target(dz, ds)
+                dest = column_target(dest_z, ds)
                 pl.when(jnp.logical_not(is_self(dest)))(
-                    lambda: act(tile_copy(tile_slot, dest, dz * sub + ds))
+                    lambda: act(tile_copy(tile_slot, dest, dest_z * sub + ds))
                 )
 
-        repeat(zs, over_columns)
+        farthest_first(over_columns)
         repeat(per_tile, over_rows)
 
     each_send(lambda copy: copy.start())

time: 20.2 us -> 19.5 us (0.965)
  Pallas kernels: 18.6 us -> 18 us
    pallas_call x1, Pallas kernels: 18.6 us -> 18 us  [shards(): pl.pallas_call(functools.partial(kernel, (zs, chan, sub, block, length)),...]
where the time goes in v4:
time: 19.5 us; the launch traced here: 19.3 us
  Pallas kernels  18 us (92%)
  local copies, waits for them, and re-layouts  1.32 us (7%)
    pallas_call x1, Pallas kernels, shards(): pl.pallas_call(functools.partial(kernel, (zs, chan, sub, block, length)),...  18 us
    unnamed x1, local copies, waits for them, and re-layouts  1.32 us

profile of v4, /device:TPU:0, one launch (start us, length us, event | category | flops | bytes accessed | tf_op | source)
XLA Modules:
  0.0 19.3 jit_solution(5382314409840083175)
XLA Ops:
  0.0 18.0 %shard_map.91 = bf16[4,16,128]{2,1,0:T(8,128)(2,1)} custom-call(bf16[4,32,128]{2,1,0:T(8,128)(2,1)} %pair_ref.1, s32[1,32]{1,0:T(1,128)} %bitcast.3, f32[2,128]{1,0:T(2,128)} %in_gain_ref.1, f32[2,128]{1,0:T(2,128)} %in_bias_ref.1, bf16[2,4,64,128]{3,2,1,0:T(8,128)(2,1)} %bitcast.2, bf16[2,128,128]{2,1,0:T(8,128)(2,1)} %gate_ref.1, f32[2,128]{1,0:T(2,128)} %out_gain_ref.1, ...), custom_call_target="tpu_custom_call" | custom-call | tf_op jit(solution)/shard_map/pallas_call | solution.py:444
  18.0 1.3 %copy.11 = bf16[4,16,128]{2,1,0:T(8,128)(2,1)} copy(bf16[4,16,128]{2,1,0:T(8,128)(2,1)} %shard_map.91) | data formatting | bytes 32768

commit v5 on v4

--- a/solution.py
+++ b/solution.py
@@ -97,6 +97,7 @@
 
     part = proj_ref.shape[2]
     own_part = pl.ds(pl.multiple_of(x * part, part), part)
+    own_rows = left_rows.at[pl.ds(s * block, block)]
 
     def farthest_first(act):
         def at_distance(step):
@@ -111,7 +112,7 @@
         pltpu.make_async_copy(source, target, local_sem.at[index])
         for index, (source, target) in enumerate(
             (
-                (pair_ref, left_rows.at[pl.ds(s * block, block)]),
+                (pair_ref, own_rows),
                 (proj_ref.at[0], full.at[0, :, own_part]),
                 (proj_ref.at[1], full.at[1, :, own_part]),
                 (in_gain_ref, in_gain),
@@ -153,13 +154,16 @@
     repeat(zs, greet)
     pl.semaphore_wait(barrier, zs * others - 1)
 
+    for copy in small:
+        copy.wait()
+
     target_tile = own_block // per_tile
     target_x, target_s = target_tile % chan, target_tile // chan
     slot = own_block % per_tile
 
     def left_copy(ds):
         return pltpu.make_async_remote_copy(
-            src_ref=pair_ref,
+            src_ref=own_rows,
             dst_ref=left_rows.at[pl.ds(s * block, block)],
             send_sem=first_send.at[zs + ds - 1],
             recv_sem=left_recv.at[s],
@@ -169,7 +173,7 @@
 
     def right_copy(dest_z):
         return pltpu.make_async_remote_copy(
-            src_ref=pair_ref,
+            src_ref=own_rows,
             dst_ref=right_rows.at[pl.ds(slot * block, block)],
             send_sem=first_send.at[dest_z],
             recv_sem=right_recv.at[slot],
@@ -182,7 +186,7 @@
 
     def piece_copy(layer, dx):
         return pltpu.make_async_remote_copy(
-            src_ref=proj_ref.at[layer],
+            src_ref=full.at[layer, :, own_part],
             dst_ref=full.at[layer, :, own_part],
             send_sem=piece_send.at[layer, dx - 1],
             recv_sem=piece_recv.at[layer, x],
@@ -208,14 +212,11 @@
     mask_col = jnp.sum(jnp.where(rows_iota == cols_iota, mask_row, 0.0), axis=1, keepdims=True)
     mask_cols[...] = jnp.broadcast_to(mask_col, mask_cols.shape)
 
-    for copy in small:
-        copy.wait()
-
     def assemble(layer):
         for other in range(1, chan):
             source = (x + other) % chan
             pltpu.make_async_remote_copy(
-                src_ref=proj_ref.at[layer],
+                src_ref=full.at[layer, :, own_part],
                 dst_ref=full.at[layer, :, pl.ds(pl.multiple_of(source * part, part), part)],
                 send_sem=piece_send.at[layer, other - 1],
                 recv_sem=piece_recv.at[layer, source],
@@ -240,7 +241,7 @@
     for ds in range(1, sub):
         source = (s + ds) % sub
         pltpu.make_async_remote_copy(
-            src_ref=pair_ref,
+            src_ref=own_rows,
             dst_ref=left_rows.at[pl.ds(source * block, block)],
             send_sem=first_send.at[zs + ds - 1],
             recv_sem=left_recv.at[source],
@@ -272,7 +273,7 @@
         @pl.when(source != own_block)
         def _():
             pltpu.make_async_remote_copy(
-                src_ref=pair_ref,
+                src_ref=own_rows,
                 dst_ref=right_rows.at[where],
                 send_sem=first_send.at[0],
                 recv_sem=right_recv.at[p],

time: 19.5 us -> 19.3 us (0.990)
  Pallas kernels: 18 us -> 17.8 us
where the time goes in v5:
time: 19.3 us; the launch traced here: 19.1 us
  Pallas kernels  17.8 us (92%)
  local copies, waits for them, and re-layouts  1.32 us (7%)
    pallas_call x1, Pallas kernels, shards(): pl.pallas_call(functools.partial(kernel, (zs, chan, sub, block, length)),...  17.8 us
    unnamed x1, local copies, waits for them, and re-layouts  1.32 us

profile of v5, /device:TPU:0, one launch (start us, length us, event | category | flops | bytes accessed | tf_op | source)
XLA Modules:
  0.0 19.1 jit_solution(12910726699119634905)
XLA Ops:
  0.0 17.8 %shard_map.91 = bf16[4,16,128]{2,1,0:T(8,128)(2,1)} custom-call(bf16[4,32,128]{2,1,0:T(8,128)(2,1)} %pair_ref.1, s32[1,32]{1,0:T(1,128)} %bitcast.3, f32[2,128]{1,0:T(2,128)} %in_gain_ref.1, f32[2,128]{1,0:T(2,128)} %in_bias_ref.1, bf16[2,4,64,128]{3,2,1,0:T(8,128)(2,1)} %bitcast.2, bf16[2,128,128]{2,1,0:T(8,128)(2,1)} %gate_ref.1, f32[2,128]{1,0:T(2,128)} %out_gain_ref.1, ...), custom_call_target="tpu_custom_call" | custom-call | tf_op jit(solution)/shard_map/pallas_call | solution.py:445
  17.8 1.3 %copy.11 = bf16[4,16,128]{2,1,0:T(8,128)(2,1)} copy(bf16[4,16,128]{2,1,0:T(8,128)(2,1)} %shard_map.91) | data formatting | bytes 32768

commit v6 on v5

--- a/solution.py
+++ b/solution.py
@@ -108,6 +108,27 @@
         repeat(zs - 1, at_distance)
         act(z)
 
+    barrier = pltpu.get_barrier_semaphore()
+    others = chan * sub
+
+    def greet(dest_z):
+        for inner in range(others):
+            dx, ds = inner // sub, inner % sub
+
+            def signal():
+                pl.semaphore_signal(
+                    barrier,
+                    inc=1,
+                    device_id=device(dest_z, (x + dx) % chan, (s + ds) % sub),
+                    device_id_type=MESH,
+                )
+
+            if inner == 0:
+                pl.when(dest_z != z)(signal)
+            else:
+                signal()
+
+    farthest_first(greet)
     small = [
         pltpu.make_async_copy(source, target, local_sem.at[index])
         for index, (source, target) in enumerate(
@@ -127,31 +148,11 @@
     for copy in small:
         copy.start()
 
-    barrier = pltpu.get_barrier_semaphore()
-    others = chan * sub
-
-    def greet(dz):
-        for inner in range(others):
-            dx, ds = inner // sub, inner % sub
-
-            def signal():
-                pl.semaphore_signal(
-                    barrier,
-                    inc=1,
-                    device_id=device((z + dz) % zs, (x + dx) % chan, (s + ds) % sub),
-                    device_id_type=MESH,
-                )
-
-            if inner == 0:
-                if isinstance(dz, int):
-                    if dz != 0:
-                        signal()
-                else:
-                    pl.when(dz != 0)(signal)
-            else:
-                signal()
-
-    repeat(zs, greet)
+    rows_iota = lax.broadcasted_iota(jnp.int32, (length, length), 0)
+    cols_iota = lax.broadcasted_iota(jnp.int32, (length, length), 1)
+    mask_row = mask_ref[...].astype(jnp.float32)
+    mask_col = jnp.sum(jnp.where(rows_iota == cols_iota, mask_row, 0.0), axis=1, keepdims=True)
+    mask_cols[...] = jnp.broadcast_to(mask_col, mask_cols.shape)
     pl.semaphore_wait(barrier, zs * others - 1)
 
     for copy in small:
@@ -194,23 +195,17 @@
             device_id_type=MESH,
         )
 
+    def start_right(dest_z):
+        pl.when(sends_right(dest_z))(lambda: right_copy(dest_z).start())
+
+    farthest_first(start_right)
     for dx in range(1, chan):
         piece_copy(0, dx).start()
-
-    def start_right(dest_z):
-        pl.when(sends_right(dest_z))(lambda: right_copy(dest_z).start())
-
-    farthest_first(start_right)
     for ds in range(1, sub):
         left_copy(ds).start()
     for dx in range(1, chan):
         piece_copy(1, dx).start()
 
-    rows_iota = lax.broadcasted_iota(jnp.int32, (length, length), 0)
-    cols_iota = lax.broadcasted_iota(jnp.int32, (length, length), 1)
-    mask_row = mask_ref[...].astype(jnp.float32)
-    mask_col = jnp.sum(jnp.where(rows_iota == cols_iota, mask_row, 0.0), axis=1, keepdims=True)
-    mask_cols[...] = jnp.broadcast_to(mask_col, mask_cols.shape)
 
     def assemble(layer):
         for other in range(1, chan):

time: 19.3 us -> 19.3 us (level)
  no operation moved by 1% of the time
where the time goes in v6:
time: 19.3 us; the launch traced here: 19.1 us
  Pallas kernels  17.8 us (92%)
  local copies, waits for them, and re-layouts  1.32 us (7%)
    pallas_call x1, Pallas kernels, shards(): pl.pallas_call(functools.partial(kernel, (zs, chan, sub, block, length)),...  17.8 us
    unnamed x1, local copies, waits for them, and re-layouts  1.32 us

profile of v6, /device:TPU:0, one launch (start us, length us, event | category | flops | bytes accessed | tf_op | source)
XLA Modules:
  0.0 19.1 jit_solution(57325512940231842)
XLA Ops:
  0.0 17.8 %shard_map.91 = bf16[4,16,128]{2,1,0:T(8,128)(2,1)} custom-call(bf16[4,32,128]{2,1,0:T(8,128)(2,1)} %pair_ref.1, s32[1,32]{1,0:T(1,128)} %bitcast.3, f32[2,128]{1,0:T(2,128)} %in_gain_ref.1, f32[2,128]{1,0:T(2,128)} %in_bias_ref.1, bf16[2,4,64,128]{3,2,1,0:T(8,128)(2,1)} %bitcast.2, bf16[2,128,128]{2,1,0:T(8,128)(2,1)} %gate_ref.1, f32[2,128]{1,0:T(2,128)} %out_gain_ref.1, ...), custom_call_target="tpu_custom_call" | custom-call | tf_op jit(solution)/shard_map/pallas_call | solution.py:440
  17.8 1.3 %copy.11 = bf16[4,16,128]{2,1,0:T(8,128)(2,1)} copy(bf16[4,16,128]{2,1,0:T(8,128)(2,1)} %shard_map.91) | data formatting | bytes 32768
